TPU v7x, 32 devices: a whole 2x2x4 slice. The times are simulated.
32 devices in a mesh: groups: 2 (over y), streams: 8 (over z, x), segment: 2 (over core).
Axes of the slice: x: 2, y: 2, z: 4, core: 2. Of those that a mesh axis runs over, the one named last changes fastest.
Arguments:
- latent: bfloat16 [4096, 1024], P(('groups', 'streams'), 'segment'), parts along dimension 0, may hold values from -6 to 6
- conv_weight: bfloat16 [1024, 16, 512], P('streams', None, 'segment'), may hold values from -0.1875 to 0.1875
- conv_bias: float32 [512], P('segment'), may hold values from -3 to 3
- tail_cache: bfloat16 [128, 8, 512], P(('groups', 'streams'), None, 'segment'), parts along dimension 0, may hold values from -6 to 6
- input_cache: bfloat16 [128, 2, 512], P(('groups', 'streams'), None, 'segment'), parts along dimension 0, may hold values from -0.8984375 to 2
- resume_slot: int32 [128], P(('groups', 'streams')), parts along dimension 0, may hold values from -1 to 255, as said below
- res_weight: bfloat16 [3, 512, 256], P(None, 'segment'), may hold values from -0.15625 to 0.15625
- res_bias: float32 [256], replicated, may hold values from -3 to 3
- skip_weight: bfloat16 [256, 512], P(None, 'segment'), may hold values from -0.375 to 0.375
- skip_bias: float32 [512], P('segment'), may hold values from -3 to 3
Outputs:
- decoded: bfloat16 [4096, 8, 512], P(('groups', 'streams'), None, 'segment'), parts along dimension 0
- new_tail: bfloat16 [4096, 8, 512], P(('groups', 'streams'), None, 'segment'), parts along dimension 0
There are 2 independent parts, one for each index of `groups`. A program takes and returns all parts, laid end to end along the dimension named above; an argument that names none is the same for every part. Nothing has to cross between parts.
Inputs may be any that keep to these rules, and one draw needn't show every extreme that they name: `resume_slot`: slot k of an owner device's store serves decoder device k // 1 of the same index range; an entry is -1 (slot unused) or the position, among that decoder device's 256 rows in decoder order, of the session that resumes from it. No decoder row is named by two slots. In every draw there is one decoder device all of whose reserved slots are in use (none is -1).
All inputs are finite; a program needn't handle non-finite values.
Results may differ from a plain program's by a relative error of at most 0.0042.
Values may be sent and summed in bfloat16 or wider, within the bound.
A program may use at most 64 MiB of HBM per device.

v0:
```python
import jax
import jax.numpy as jnp
from jax import lax
from jax.sharding import PartitionSpec as P


def apply_elu(values):
    return jnp.where(values > 0, values, jnp.expm1(jnp.minimum(values, 0.0)))


def local(
    latent,
    conv_weight,
    conv_bias,
    tail_cache,
    input_cache,
    resume_slot,
    res_weight,
    res_bias,
    skip_weight,
    skip_bias,
):
    handed = lax.all_to_all(latent, "streams", split_axis=0, concat_axis=0, tiled=True)
    excitation_half = apply_elu(handed.astype(jnp.float32)).astype(jnp.bfloat16)
    excitation = lax.all_gather(excitation_half, "segment", axis=1, tiled=True)
    session_rows = excitation.shape[0]
    tap_count = conv_weight.shape[1]
    half_taps = tap_count // 2
    half_width = conv_weight.shape[2]
    piece = lax.all_gather(conv_weight, "streams", axis=0, tiled=True)
    kernel_rows = piece.reshape(piece.shape[0], tap_count * half_width)
    spread = jnp.dot(excitation, kernel_rows, preferred_element_type=jnp.float32)
    spread = spread.reshape(session_rows, tap_count, half_width)
    fetched_tail, fetched_input, fetched_slot = (
        lax.all_to_all(tail_cache, "streams", split_axis=0, concat_axis=0, tiled=True),
        lax.all_to_all(input_cache, "streams", split_axis=0, concat_axis=0, tiled=True),
        lax.all_to_all(resume_slot, "streams", split_axis=0, concat_axis=0, tiled=True),
    )
    arrivals = fetched_slot.shape[0]
    state_steps = fetched_input.shape[1]
    packed = jnp.concatenate(
        [fetched_tail.reshape(arrivals, -1), fetched_input.reshape(arrivals, -1)], axis=1
    )
    one_hot = (fetched_slot[None, :] == jnp.arange(session_rows, dtype=jnp.int32)[:, None]).astype(
        jnp.bfloat16
    )
    placed = jnp.dot(one_hot, packed, preferred_element_type=jnp.float32)
    prev_tail = placed[:, : half_taps * half_width].reshape(session_rows, half_taps, half_width)
    prev_input = (
        placed[:, half_taps * half_width :]
        .reshape(session_rows, state_steps, half_width)
        .astype(jnp.bfloat16)
    )
    upsampled = spread[:, :half_taps] + prev_tail + conv_bias
    new_tail = spread[:, half_taps:].astype(jnp.bfloat16)
    excited = apply_elu(upsampled).astype(jnp.bfloat16)
    window = jnp.concatenate([prev_input, excited], axis=1)
    hidden_width = res_weight.shape[2]
    partial_value = jnp.zeros((session_rows * half_taps, hidden_width), jnp.float32)
    for offset in range(res_weight.shape[0]):
        frames = window[:, offset : offset + half_taps].reshape(
            session_rows * half_taps, half_width
        )
        partial_value = partial_value + jnp.dot(
            frames, res_weight[offset], preferred_element_type=jnp.float32
        )
    partial_value = partial_value.reshape(session_rows, half_taps, hidden_width)
    summed = lax.psum(partial_value, "segment")
    hidden = apply_elu(summed + res_bias).astype(jnp.bfloat16)
    projected = jnp.dot(
        hidden.reshape(session_rows * half_taps, hidden_width),
        skip_weight,
        preferred_element_type=jnp.float32,
    )
    decoded_block = upsampled + projected.reshape(session_rows, half_taps, half_width) + skip_bias
    return (decoded_block.astype(jnp.bfloat16), new_tail)


def solution(mesh):
    placed = (
        P(("groups", "streams"), "segment"),
        P("streams", None, "segment"),
        P("segment"),
        P(("groups", "streams"), None, "segment"),
        P(("groups", "streams"), None, "segment"),
        P(("groups", "streams")),
        P(None, "segment", None),
        P(),
        P(None, "segment"),
        P("segment"),
    )
    return jax.shard_map(
        local,
        mesh=mesh,
        in_specs=placed,
        out_specs=(
            P(("groups", "streams"), None, "segment"),
            P(("groups", "streams"), None, "segment"),
        ),
        check_vma=False,
    )
```

profile of v0, /device:TPU:0, one launch (start us, length us, event | category | flops | bytes accessed | tf_op | source)
XLA Modules:
  0.0 200.5 jit_solution(6672146681331437145)
XLA Ops:
  7.2 0.7 all-gather.2.cloned.1.call-update
  7.9 0.7 copy.39
  8.6 13.6 %all_to_all.28 = s32[8,1,1]{2,1,0:T(1,128)S(1)} all-to-all(s32[8,1,1]{2,1,0:T(1,128)S(1)} %copy.39), channel_id=1, replica_groups=mesh['groups'=2,'streams'=8,'segment'=2] {'streams'}, dimensions={0} | all-to-all | bytes 64 | tf_op jit(solution)/shard_map/all_to_all | solution.py:37
  22.2 10.1 %all_to_all.29 = bf16[8,2,256]{2,1,0:T(2,128)(2,1)S(1)} all-to-all(bf16[8,2,256]{2,1,0:T(2,128)(2,1)} %param.14), channel_id=1, replica_groups=mesh['groups'=2,'streams'=8,'segment'=2] {'streams'}, dimensions={0} | all-to-all | bytes 16384 | tf_op jit(solution)/shard_map/all_to_all | solution.py:36
  32.3 10.5 %all_to_all.30 = bf16[8,8,256]{2,1,0:T(8,128)(2,1)S(1)} all-to-all(bf16[8,8,256]{2,1,0:T(8,128)(2,1)} %param.13), channel_id=1, replica_groups=mesh['groups'=2,'streams'=8,'segment'=2] {'streams'}, dimensions={0} | all-to-all | bytes 65536 | tf_op jit(solution)/shard_map/all_to_all | solution.py:35
  42.8 3.4 %all-to-all-start = ((bf16[8,32,512]{2,1,0:T(8,128)(2,1)}), bf16[8,32,512]{2,1,0:T(8,128)(2,1)S(1)}, u32[]{:S(2)}, u32[]{:S(2)}) async-start(bf16[8,32,512]{2,1,0:T(8,128)(2,1)} %bitcast.46), calls=%async_computation | async-start | bytes 524288 | tf_op jit(solution)/shard_map/all_to_all | solution.py:23
  46.3 0.2 reduce
  46.5 0.5 fusion.27
  47.1 0.2 slice.39
  47.2 1.9 copy.40
  49.1 1.9 copy.41
  51.0 0.1 copy.42
  51.2 0.1 copy.43
  51.3 10.6 %all-to-all-done = bf16[8,32,512]{2,1,0:T(8,128)(2,1)S(1)} async-done(((bf16[8,32,512]{2,1,0:T(8,128)(2,1)}), bf16[8,32,512]{2,1,0:T(8,128)(2,1)S(1)}, u32[]{:S(2)}, u32[]{:S(2)}) %all-to-all-start) | async-done | bytes 262176 | tf_op jit(solution)/shard_map/all_to_all | solution.py:23
  61.9 0.2 fusion.18
  62.1 2.4 %all_gather.6 = bf16[256,1024]{1,0:T(8,128)(2,1)S(1)} all-gather(bf16[256,512]{1,0:T(8,128)(2,1)S(1)} %fusion.18), channel_id=1, replica_groups=mesh['groups'=2,'streams'=8,'segment'=2] {'segment'}, dimensions={1}, use_global_device_ids=true | all-gather | bytes 786432 | tf_op jit(solution)/shard_map/all_gather | solution.py:25
  64.5 79.3 %all-gather.2.cloned.1.call-done = bf16[1024,16,256]{2,1,0:T(8,128)(2,1)} async-done(((bf16[128,16,256]{2,1,0:T(8,128)(2,1)}), bf16[1024,16,256]{2,1,0:T(8,128)(2,1)}) %all-gather.2.cloned.1.call-update) | async-done | bytes 8388624 | tf_op jit(solution)/shard_map/all_gather | solution.py:30
  143.7 12.3 %copy.50 = bf16[1024,16,256]{0,2,1:T(8,128)(2,1)} copy(bf16[1024,16,256]{2,1,0:T(8,128)(2,1)} %all-gather.2.cloned.1.call-done) | data formatting | bytes 16777216 | tf_op jit(solution)/shard_map/reshape | solution.py:31
  156.0 5.8 %fusion = f32[256,16,256]{2,0,1:T(8,128)S(1)} fusion(bf16[1024,16,256]{0,2,1:T(8,128)(2,1)} %copy.50, bf16[256,1024]{1,0:T(8,128)(2,1)S(1)} %all_gather.6), kind=kOutput, calls=%fused_computation | convolution fusion | flops 2147483648 | bytes 13107200 | tf_op jit(solution)/shard_map/dot_general | solution.py:32
  161.8 1.0 fusion.2
  162.7 1.0 copy-done.1
  163.7 0.1 pad_maximum_fusion
  163.9 0.9 copy-done.2
  164.7 0.7 fusion.10
  165.4 0.8 convolution_add_fusion.1
  166.2 0.8 fusion.5
  167.0 2.0 copy.47
  169.0 1.7 slice.71
  170.8 1.6 copy.49
  172.3 16.3 %all-reduce.2.cloned.1.call-done = f32[256,8,256]{2,0,1:T(8,128)} async-done(((f32[256,8,256]{2,0,1:T(8,128)}), f32[256,8,256]{2,0,1:T(8,128)}) %all-reduce.2.cloned.1.call-update) | async-done | bytes 2097168 | tf_op jit(solution)/shard_map/psum | solution.py:68
  188.7 3.4 %add_convert_fusion = bf16[256,8,256]{2,0,1:T(8,128)(2,1)S(1)} fusion(f32[256,8,256]{2,0,1:T(8,128)} %all-reduce.2.cloned.1.call-done, f32[256]{0:T(256)S(1)} %copy-done.4, f32[256]{0:T(256)S(1)} %copy-done.5, f32[256]{0:T(256)S(1)} %copy-done.3, f32[256,8,256]{2,0,1:T(8,128)S(1)} %copy.41, f32[256,16,256]{2,0,1:T(8,128)} %copy-done.1, ...), kind=kOutput, calls=%fused_computation.11 | convolution fusion | flops 273678336 | bytes 7474176 | tf_op jit(solution)/shard_map/dot_general | solution.py:70
  192.1 1.6 copy.48
  (16 shorter events, 0.2 us)
Async XLA Ops:
  7.2 181.5 %copy-start = (bf16[256,256]{1,0:T(8,128)(2,1)S(1)}, bf16[256,256]{1,0:T(8,128)(2,1)}, u32[]{:S(2)}) copy-start(bf16[256,256]{1,0:T(8,128)(2,1)} %param.18) | copy-start | bytes 393220
  7.2 136.5 %all-gather.2.cloned.1.call-start = ((), (), s32[]{:S(2)}) async-start(), calls=%async_computation.4 | async-start | bytes 9437184 | tf_op jit(solution)/shard_map/all_gather | solution.py:30
  42.8 19.1 %all-to-all-start = ((bf16[8,32,512]{2,1,0:T(8,128)(2,1)}), bf16[8,32,512]{2,1,0:T(8,128)(2,1)S(1)}, u32[]{:S(2)}, u32[]{:S(2)}) async-start(bf16[8,32,512]{2,1,0:T(8,128)(2,1)} %bitcast.46), calls=%async_computation | async-start | bytes 524288 | tf_op jit(solution)/shard_map/all_to_all | solution.py:23
  46.2 142.4 %all-reduce.2.cloned.1.call-start = ((), (), s32[]{:S(2)}) async-start(), calls=%async_computation.5 | async-start | bytes 4194304 | tf_op jit(solution)/shard_map/psum | solution.py:68
  156.0 5.8 %copy-start.3 = (f32[256]{0:T(256)S(1)}, f32[256]{0:T(256)}, u32[]{:S(2)}) copy-start(f32[256]{0:T(256)} %param.12) | copy-start | bytes 3076
  161.8 1.9 copy-start.1
  163.7 1.0 copy-start.2
  169.0 19.6 %copy-start.4 = (f32[256]{0:T(256)S(1)}, f32[256]{0:T(256)}, u32[]{:S(2)}) copy-start(f32[256]{0:T(256)} %param.19) | copy-start | bytes 3076
  169.0 19.6 %copy-start.5 = (f32[256]{0:T(256)S(1)}, f32[256]{0:T(256)}, u32[]{:S(2)}) copy-start(f32[256]{0:T(256)} %param.17) | copy-start | bytes 3076
Sparse Core Ops, SparseCore 0:
  10.1 133.5 all-gather.1
  169.1 19.4 all-reduce.1
where the time goes:
time: 201 us; the launch traced here: 200 us
  waiting for transfers between devices  107 us (53%)
  blocking collectives  36.5 us (18%)
  local copies, waits for them, and re-layouts  25.9 us (13%)
  between operations  14.2 us (7%)
  matrix products  11.9 us (6%)
  starting transfers between devices  3.49 us (2%)
    all_gather x1, waiting for transfers between devices, local(): piece = lax.all_gather(conv_weight, 'streams', axis=0, tiled=True)  79.3 us
    psum x1, waiting for transfers between devices, local(): summed = lax.psum(partial_value, 'segment')  16.3 us
    all_to_all x1, blocking collectives, local(): lax.all_to_all(resume_slot, 'streams', split_axis=0, concat_axis=0, tiled...  13.6 us
    reshape x1, local copies, waits for them, and re-layouts, local(): kernel_rows = piece.reshape(piece.shape[0], tap_count * half_width)  12.3 us
    all_to_all x1, waiting for transfers between devices, local(): lax.all_to_all(latent, 'streams', split_axis=0, concat_axis=0, tiled=True)  10.6 us
    all_to_all x1, blocking collectives, local(): lax.all_to_all(tail_cache, 'streams', split_axis=0, concat_axis=0, tiled=...  10.5 us
    all_to_all x1, blocking collectives, local(): lax.all_to_all(input_cache, 'streams', split_axis=0, concat_axis=0, tiled...  10.1 us
    dot_general x1, matrix products, local(): jnp.dot(excitation, kernel_rows, preferred_element_type=jnp.float32)  5.76 us
  transfers between devices with their start and end apart: 3, of which 3 were waited for; matrix products, arithmetic and copies ran while one was open for 5% of the time, Pallas kernels for 0%

commit v1 on v0

--- a/solution.py
+++ b/solution.py
@@ -2,6 +2,7 @@
 import jax.numpy as jnp
 from jax import lax
 from jax.sharding import PartitionSpec as P
+from jax.lax import all_gather
 
 
 def apply_elu(values):
@@ -65,7 +66,7 @@
             frames, res_weight[offset], preferred_element_type=jnp.float32
         )
     partial_value = partial_value.reshape(session_rows, half_taps, hidden_width)
-    summed = lax.psum(partial_value, "segment")
+    summed = jnp.sum(all_gather(partial_value, "segment"), axis=0)
     hidden = apply_elu(summed + res_bias).astype(jnp.bfloat16)
     projected = jnp.dot(
         hidden.reshape(session_rows * half_taps, hidden_width),

time: 201 us -> 197 us (0.980)
  waiting for transfers between devices: 107 us -> 99.2 us
  other arithmetic: 1.57 us -> 5.65 us
    psum x1 -> x0, waiting for transfers between devices: 16.3 us -> none  [local(): summed = lax.psum(partial_value, 'segment')]
    all_gather x0 -> x1, waiting for transfers between devices: none -> 8.72 us  [local(): summed = jnp.sum(all_gather(partial_value, 'segment'), axis=0)]
    reduce_sum x0 -> x1, other arithmetic: none -> 4.08 us  [local(): summed = jnp.sum(all_gather(partial_value, 'segment'), axis=0)]
where the time goes in v1:
time: 197 us
  waiting for transfers between devices  99.2 us (50%)
  blocking collectives  36.5 us (19%)
  local copies, waits for them, and re-layouts  23.9 us (12%)
  between operations  14.2 us (7%)
  matrix products  13.5 us (7%)
  other arithmetic  5.65 us (3%)
  starting transfers between devices  3.49 us (2%)
    all_gather x1, waiting for transfers between devices, local(): piece = lax.all_gather(conv_weight, 'streams', axis=0, tiled=True)  79.3 us
    all_to_all x1, blocking collectives, local(): lax.all_to_all(resume_slot, 'streams', split_axis=0, concat_axis=0, tiled...  13.6 us
    reshape x1, local copies, waits for them, and re-layouts, local(): kernel_rows = piece.reshape(piece.shape[0], tap_count * half_width)  12.3 us
    all_to_all x1, waiting for transfers between devices, local(): lax.all_to_all(latent, 'streams', split_axis=0, concat_axis=0, tiled=True)  10.6 us
    all_to_all x1, blocking collectives, local(): lax.all_to_all(tail_cache, 'streams', split_axis=0, concat_axis=0, tiled=...  10.5 us
    all_to_all x1, blocking collectives, local(): lax.all_to_all(input_cache, 'streams', split_axis=0, concat_axis=0, tiled...  10.1 us
    all_gather x1, waiting for transfers between devices, local(): summed = jnp.sum(all_gather(partial_value, 'segment'), axis=0)  8.72 us
    dot_general x1, matrix products, local(): jnp.dot(excitation, kernel_rows, preferred_element_type=jnp.float32)  5.76 us
  transfers between devices with their start and end apart: 3, of which 3 were waited for; matrix products, arithmetic and copies ran while one was open for 5% of the time, Pallas kernels for 0%

profile of v1, /device:TPU:0, one launch (start us, length us, event | category | flops | bytes accessed | tf_op | source)
XLA Modules:
  0.0 196.5 jit_solution(5465649629616151837)
XLA Ops:
  7.2 0.7 all-gather.3.cloned.1.call-update
  7.9 0.7 copy.38
  8.6 13.6 %all_to_all.28 = s32[8,1,1]{2,1,0:T(1,128)S(1)} all-to-all(s32[8,1,1]{2,1,0:T(1,128)S(1)} %copy.38), channel_id=1, replica_groups=mesh['groups'=2,'streams'=8,'segment'=2] {'streams'}, dimensions={0} | all-to-all | bytes 64 | tf_op jit(solution)/shard_map/all_to_all | solution.py:38
  22.2 10.1 %all_to_all.29 = bf16[8,2,256]{2,1,0:T(2,128)(2,1)S(1)} all-to-all(bf16[8,2,256]{2,1,0:T(2,128)(2,1)} %param.14), channel_id=1, replica_groups=mesh['groups'=2,'streams'=8,'segment'=2] {'streams'}, dimensions={0} | all-to-all | bytes 16384 | tf_op jit(solution)/shard_map/all_to_all | solution.py:37
  32.3 10.5 %all_to_all.30 = bf16[8,8,256]{2,1,0:T(8,128)(2,1)S(1)} all-to-all(bf16[8,8,256]{2,1,0:T(8,128)(2,1)} %param.13), channel_id=1, replica_groups=mesh['groups'=2,'streams'=8,'segment'=2] {'streams'}, dimensions={0} | all-to-all | bytes 65536 | tf_op jit(solution)/shard_map/all_to_all | solution.py:36
  42.8 3.4 %all-to-all-start = ((bf16[8,32,512]{2,1,0:T(8,128)(2,1)}), bf16[8,32,512]{2,1,0:T(8,128)(2,1)S(1)}, u32[]{:S(2)}, u32[]{:S(2)}) async-start(bf16[8,32,512]{2,1,0:T(8,128)(2,1)} %bitcast.46), calls=%async_computation | async-start | bytes 524288 | tf_op jit(solution)/shard_map/all_to_all | solution.py:24
  46.3 0.2 reduce
  46.5 0.5 fusion.27
  47.1 0.2 slice.39
  47.2 1.9 copy.39
  49.1 1.9 copy.40
  51.0 0.1 copy.41
  51.2 0.1 copy.42
  51.3 10.6 %all-to-all-done = bf16[8,32,512]{2,1,0:T(8,128)(2,1)S(1)} async-done(((bf16[8,32,512]{2,1,0:T(8,128)(2,1)}), bf16[8,32,512]{2,1,0:T(8,128)(2,1)S(1)}, u32[]{:S(2)}, u32[]{:S(2)}) %all-to-all-start) | async-done | bytes 262176 | tf_op jit(solution)/shard_map/all_to_all | solution.py:24
  61.9 0.2 fusion.18
  62.1 2.4 %all_gather.9 = bf16[256,1024]{1,0:T(8,128)(2,1)S(1)} all-gather(bf16[256,512]{1,0:T(8,128)(2,1)S(1)} %fusion.18), channel_id=1, replica_groups=mesh['groups'=2,'streams'=8,'segment'=2] {'segment'}, dimensions={1}, use_global_device_ids=true | all-gather | bytes 786432 | tf_op jit(solution)/shard_map/all_gather | solution.py:26
  64.5 79.3 %all-gather.3.cloned.1.call-done = bf16[1024,16,256]{2,1,0:T(8,128)(2,1)} async-done(((bf16[128,16,256]{2,1,0:T(8,128)(2,1)}), bf16[1024,16,256]{2,1,0:T(8,128)(2,1)}) %all-gather.3.cloned.1.call-update) | async-done | bytes 8388624 | tf_op jit(solution)/shard_map/all_gather | solution.py:31
  143.7 12.3 %copy.49 = bf16[1024,16,256]{0,2,1:T(8,128)(2,1)} copy(bf16[1024,16,256]{2,1,0:T(8,128)(2,1)} %all-gather.3.cloned.1.call-done) | data formatting | bytes 16777216 | tf_op jit(solution)/shard_map/reshape | solution.py:32
  156.0 5.8 %fusion = f32[256,16,256]{2,0,1:T(8,128)S(1)} fusion(bf16[1024,16,256]{0,2,1:T(8,128)(2,1)} %copy.49, bf16[256,1024]{1,0:T(8,128)(2,1)S(1)} %all_gather.9), kind=kOutput, calls=%fused_computation | convolution fusion | flops 2147483648 | bytes 13107200 | tf_op jit(solution)/shard_map/dot_general | solution.py:33
  161.8 1.0 fusion.2
  162.7 1.0 copy-done.1
  163.7 0.1 pad_maximum_fusion
  163.9 0.9 copy-done.2
  164.7 0.7 fusion.10
  165.4 0.8 convolution_add_fusion.1
  166.2 2.2 %fusion.5 = f32[1,256,8,256]{3,2,1,0:T(8,128)} fusion(f32[2048,256]{1,0:T(8,128)S(1)} %convolution_add_fusion.1, bf16[256,8,256]{2,0,1:T(8,128)(2,1)S(1)} %fusion.2, bf16[3,256,256]{2,1,0:T(8,128)(2,1)S(1)} %copy-done.2), kind=kOutput, calls=%fused_computation.13 | convolution fusion | flops 268959744 | bytes 5373952 | tf_op jit(solution)/shard_map/dot_general | solution.py:65
  168.4 1.7 slice.71
  170.1 1.6 copy.48
  171.7 8.7 %all-gather.5.cloned.1.call-done = f32[2,256,8,256]{3,2,1,0:T(8,128)} async-done(((f32[1,256,8,256]{3,2,1,0:T(8,128)}), f32[2,256,8,256]{3,2,1,0:T(8,128)}) %all-gather.5.cloned.1.call-update) | async-done | bytes 4194320 | tf_op jit(solution)/shard_map/all_gather | solution.py:69
  180.4 4.1 %reduce_sum.9 = f32[256,8,256]{2,1,0:T(8,128)} reduce(f32[2,256,8,256]{3,2,1,0:T(8,128)} %all-gather.5.cloned.1.call-done, f32[]{:T(128)} %constant.1.clone.1), dimensions={0}, to_apply=%region_0.1 | reduce | flops 524288 | bytes 6291460 | tf_op jit(solution)/shard_map/reduce_sum | solution.py:69
  184.5 3.6 %add_convert_fusion = bf16[256,8,256]{2,0,1:T(8,128)(2,1)S(1)} fusion(f32[256,8,256]{2,1,0:T(8,128)} %reduce_sum.9, f32[256]{0:T(256)S(1)} %copy-done.4, f32[256]{0:T(256)S(1)} %copy-done.5, f32[256]{0:T(256)S(1)} %copy-done.3, f32[256,8,256]{2,0,1:T(8,128)S(1)} %copy.40, f32[256,16,256]{2,0,1:T(8,128)} %copy-done.1, bf16[256,256]{1,0:T(8,128)(2,1)S(1)} %copy-done), kind=kOutput, calls=%fused_computation.12 | convolution fusion | flops 273678336 | bytes 7474176 | tf_op jit(solution)/shard_map/dot_general | solution.py:71
  188.2 1.6 copy.47
  (16 shorter events, 0.2 us)
Async XLA Ops:
  7.2 177.3 %copy-start = (bf16[256,256]{1,0:T(8,128)(2,1)S(1)}, bf16[256,256]{1,0:T(8,128)(2,1)}, u32[]{:S(2)}) copy-start(bf16[256,256]{1,0:T(8,128)(2,1)} %param.18) | copy-start | bytes 393220
  7.2 136.5 %all-gather.3.cloned.1.call-start = ((), (), s32[]{:S(2)}) async-start(), calls=%async_computation.4 | async-start | bytes 9437184 | tf_op jit(solution)/shard_map/all_gather | solution.py:31
  42.8 19.1 %all-to-all-start = ((bf16[8,32,512]{2,1,0:T(8,128)(2,1)}), bf16[8,32,512]{2,1,0:T(8,128)(2,1)S(1)}, u32[]{:S(2)}, u32[]{:S(2)}) async-start(bf16[8,32,512]{2,1,0:T(8,128)(2,1)} %bitcast.46), calls=%async_computation | async-start | bytes 524288 | tf_op jit(solution)/shard_map/all_to_all | solution.py:24
  46.2 134.2 %all-gather.5.cloned.1.call-start = ((), (), s32[]{:S(2)}) async-start(), calls=%async_computation.5 | async-start | bytes 6291456 | tf_op jit(solution)/shard_map/all_gather | solution.py:69
  156.0 5.8 %copy-start.3 = (f32[256]{0:T(256)S(1)}, f32[256]{0:T(256)}, u32[]{:S(2)}) copy-start(f32[256]{0:T(256)} %param.12) | copy-start | bytes 3076
  161.8 1.9 copy-start.1
  163.7 1.0 copy-start.2
  171.7 12.8 %copy-start.4 = (f32[256]{0:T(256)S(1)}, f32[256]{0:T(256)}, u32[]{:S(2)}) copy-start(f32[256]{0:T(256)} %param.19) | copy-start | bytes 3076
  171.7 12.8 %copy-start.5 = (f32[256]{0:T(256)S(1)}, f32[256]{0:T(256)}, u32[]{:S(2)}) copy-start(f32[256]{0:T(256)} %param.17) | copy-start | bytes 3076
Sparse Core Ops, SparseCore 0:
  10.1 133.5 all-gather.2
  168.5 11.8 all-gather.4
